TPU v7x, 32 devices: a whole 2x2x4 slice. The times are simulated.
32 devices in a mesh: groups: 2 (over x), stem: 8 (over z, y), cuts: 2 (over core).
Axes of the slice: x: 2, y: 2, z: 4, core: 2. Of those that a mesh axis runs over, the one named last changes fastest.
Arguments:
- stem: bfloat16 [4, 2, 4096, 1024], P(('groups', 'cuts'), None, 'stem'), parts along dimension 0, may hold values from -6 to 6
- edge_values: int32 [4, 4], P(('groups', 'cuts')), parts along dimension 0, may hold values from 0 to 1
- index_order: int32 [1024], replicated, may hold values from 0 to 1023, each once
- branch_first: bfloat16 [2, 1024, 1024], replicated, may hold values from -0.125 to 0.125
- branch_second: bfloat16 [2, 1024, 1024], replicated, may hold values from -0.125 to 0.125
- branch_third: bfloat16 [2, 1024, 256], replicated, may hold values from -0.125 to 0.125
- edge_table: float32 [16, 2, 256], replicated, may hold values from -6 to 6
- picks: int32 [4096], P('stem'), may hold values from 0 to 511, as said below
Outputs:
- amplitudes: float32 [2, 8192, 256], P(None, ('groups', 'stem')), parts along dimension 1
There are 2 independent parts, one for each index of `groups`. A program takes and returns all parts, laid end to end along the dimension named above; an argument that names none is the same for every part. Nothing has to cross between parts.
Inputs may be any that keep to these rules, and one draw needn't show every extreme that they name: `index_order`: each number of 0 to 1023 once. `picks`: each aligned block of 512 entries names every number of 0 to 511 once.
All inputs are finite; a program needn't handle non-finite values.
Results may differ from a plain program's by a relative error of at most 0.0041.
Values may be sent and summed in bfloat16 or wider, within the bound.
No kernel may reach another device: no remote copies, remote signals or barrier semaphores. Data moves between devices by JAX's collectives and lax.ppermute only.
A program may use at most 64 MiB of HBM per device.

v0:
```python
import jax
import jax.numpy as jnp
from jax import lax
from jax.sharding import PartitionSpec as P


def swapped(value, axis, distance):
    mask = 2**distance
    pairs = [(source, source ^ mask) for source in range(lax.axis_size(axis))]
    return lax.ppermute(value, axis, pairs)


def complex_dot(operand, matrix):
    real = jnp.dot(operand[0], matrix[0], preferred_element_type=jnp.float32) - jnp.dot(
        operand[1], matrix[1], preferred_element_type=jnp.float32
    )
    imag = jnp.dot(operand[0], matrix[1], preferred_element_type=jnp.float32) + jnp.dot(
        operand[1], matrix[0], preferred_element_type=jnp.float32
    )
    return jnp.stack([real, imag])


def on_device(
    stem, edge_values, index_order, branch_first, branch_second, branch_third, edge_table, picks
):
    stem_size = lax.axis_size("stem")
    bit_pos = stem_size.bit_length() - 2
    top_bit = lax.axis_index("stem") // (stem_size // 2) % 2
    is_low = top_bit == 0
    width = branch_first.shape[1]
    half_width = width // 2
    rows_dev = stem.shape[2]
    block_rows = rows_dev // stem_size
    inverse = jnp.zeros_like(index_order).at[index_order].set(jnp.arange(width, dtype=jnp.int32))
    reordered = jnp.take(branch_second, inverse, axis=1)
    powers = 2 ** jnp.arange(edge_values.shape[1], dtype=jnp.int32)
    codes = jnp.arange(edge_table.shape[0], dtype=jnp.int32)
    first = complex_dot(stem[0], branch_first).astype(jnp.bfloat16)
    low_half = first[:, :, :half_width]
    high_half = first[:, :, half_width:]
    outgoing = jnp.where(is_low, high_half, low_half)
    incoming = swapped(outgoing, "stem", bit_pos)
    joined = jnp.where(
        is_low,
        jnp.concatenate([low_half, incoming], axis=2),
        jnp.concatenate([incoming, high_half], axis=2),
    )
    second = complex_dot(joined, reordered).astype(jnp.bfloat16)
    contracted = complex_dot(second, branch_third)
    moved = lax.all_to_all(
        contracted.reshape(2, stem_size, block_rows, contracted.shape[2]),
        "stem",
        split_axis=1,
        concat_axis=1,
        tiled=True,
    )
    third = jnp.take(moved.reshape(2, rows_dev, contracted.shape[2]), picks, axis=1)
    code = jnp.sum(edge_values[0] * powers)
    onehot = (codes == code).astype(jnp.float32)
    factor = jnp.sum(onehot[:, None, None] * edge_table, axis=0)
    real = third[0] * factor[0][None, :] - third[1] * factor[1][None, :]
    imag = third[0] * factor[1][None, :] + third[1] * factor[0][None, :]
    total = jnp.stack([real, imag])
    return lax.psum(total, "cuts")


def solution(mesh):
    return jax.shard_map(
        on_device,
        mesh=mesh,
        in_specs=(
            P(("groups", "cuts"), None, "stem", None),
            P(("groups", "cuts"), None),
            P(),
            P(),
            P(),
            P(),
            P(),
            P("stem"),
        ),
        out_specs=P(None, ("groups", "stem"), None),
        check_vma=False,
    )
```

profile of v0, /device:TPU:0, one launch (start us, length us, event | category | flops | bytes accessed | tf_op | source)
XLA Modules:
  0.0 144.1 jit_solution(4913342444032320021)
XLA Ops:
  6.5 4.6 %fusion.2 = f32[512,1024]{1,0:T(8,128)} fusion(bf16[2,1024,1024]{2,1,0:T(8,128)(2,1)} %param.11, bf16[1,2,512,1024]{3,2,1,0:T(8,128)(2,1)} %param.8), kind=kOutput, calls=%fused_computation.11 | convolution fusion | flops 1073741824 | bytes 5242880 | tf_op jit(solution)/shard_map/dot_general | solution.py:14
  11.2 2.6 %fusion = f32[512,1024]{1,0:T(8,128)} fusion(bf16[2,1024,1024]{2,1,0:T(8,128)(2,1)S(1)} %copy-done.4, bf16[1,2,512,1024]{3,2,1,0:T(8,128)(2,1)S(1)} %copy-done.6), kind=kOutput, calls=%fused_computation.9 | convolution fusion | flops 1073741824 | bytes 5242880 | tf_op jit(solution)/shard_map/dot_general | solution.py:17
  13.8 3.6 %fusion.20 = bf16[1,512,1024]{2,1,0:T(8,128)(2,1)S(1)} fusion(f32[512,1024]{1,0:T(8,128)} %fusion.2, bf16[2,1024,1024]{2,1,0:T(8,128)(2,1)} %param.11, bf16[1,2,512,1024]{3,2,1,0:T(8,128)(2,1)S(1)} %copy-done.6), kind=kOutput, calls=%fused_computation.29 | convolution fusion | flops 1074790400 | bytes 6291456 | tf_op jit(solution)/shard_map/dot_general | solution.py:14
  17.9 1.3 fusion.23
  19.7 4.1 %collective-permute-start = (bf16[2,512,512]{2,1,0:T(8,128)(2,1)S(1)}, bf16[2,512,512]{2,1,0:T(8,128)(2,1)}, u32[]{:S(2)}, u32[]{:S(2)}) collective-permute-start(bf16[2,512,512]{2,1,0:T(8,128)(2,1)S(1)} %get-tuple-element.5), channel_id=1, source_target_pairs={{0,8},{2,10},{4,12},{6,14},{8,0},{10,2},{12,4},{14,6},{1,9},{3,11}... | collective-permute-start | bytes 3145736 | tf_op jit(solution)/shard_map/ppermute | solution.py:10
  23.8 4.5 %scatter_custom_fusion = s32[1024]{0:T(1024)S(1)} fusion(s32[1024]{0:T(1024)S(1)} %compare_select_fusion.1, s32[1024]{0:T(1024)S(1)} %iota.11, s32[]{:T(128)} %constant.69.clone.1), kind=kCustom, calls=%fused_computation.69 | custom fusion | bytes 4100 | tf_op jit(solution)/shard_map/scatter | solution.py:34
  28.3 27.6 %gather_fusion = bf16[1024,2,1024]{2,0,1:T(8,128)(2,1)} fusion(bf16[2,1024,1024]{2,1,0:T(8,128)(2,1)} %param.12, s32[1024]{0:T(1024)S(1)} %fusion.46), kind=kCustom, calls=%fused_computation | custom fusion | bytes 8392704 | tf_op jit(solution)/shard_map/jit(_take)/gather | solution.py:35
  56.0 2.6 %select_bitcast_fusion = bf16[2,1024,1024]{2,1,0:T(8,128)(2,1)S(1)} fusion(bf16[1024,2,1024]{2,0,1:T(8,128)(2,1)} %gather_fusion, pred[1024]{0:T(1024)(128)(4,1)S(1)} %compare_and_fusion), kind=kLoop, calls=%fused_computation.3 | loop fusion | flops 2097152 | bytes 8389632 | tf_op jit(solution)/shard_map/jit(_take)/select_n | solution.py:35
  58.6 10.9 %collective-permute-done = bf16[2,512,512]{2,1,0:T(8,128)(2,1)} collective-permute-done((bf16[2,512,512]{2,1,0:T(8,128)(2,1)S(1)}, bf16[2,512,512]{2,1,0:T(8,128)(2,1)}, u32[]{:S(2)}, u32[]{:S(2)}) %collective-permute-start) | collective-permute-done | bytes 1048608 | tf_op jit(solution)/shard_map/ppermute | solution.py:10
  69.6 2.2 %maximum_select_fusion = bf16[2,512,1024]{2,1,0:T(8,128)(2,1)S(1)} fusion(bf16[2,512,512]{2,1,0:T(8,128)(2,1)} %collective-permute-done, bf16[2,512,512]{2,1,0:T(8,128)(2,1)S(1)} %get-tuple-element.6, bf16[2,512,512]{2,1,0:T(8,128)(2,1)S(1)} %get-tuple-element.7, pred[]{:T(512)S(6)} %eq.15), kind=kLoop, calls=%fused_computation.8 | loop fusion | flops 9437184 | bytes 5242881 | tf_op jit(solution)/shard_map/jit(_where)/select_n | solution.py:43
  71.8 1.3 fusion.8
  73.1 1.3 fusion.11
  74.3 1.3 subtract_convert_fusion
  76.6 1.3 add_convert_fusion
  78.8 1.1 pad_maximum_fusion.1
  79.9 5.8 %all-to-all-start = ((f32[2,8,64,256]{3,2,0,1:T(8,128)}), f32[2,8,64,256]{3,2,0,1:T(8,128)S(1)}, u32[]{:S(2)}, u32[]{:S(2)}) async-start(f32[2,8,64,256]{3,2,0,1:T(8,128)} %pad_maximum_fusion.1), calls=%async_computation | async-start | bytes 2097152 | tf_op jit(solution)/shard_map/all_to_all | solution.py:50
  85.7 0.6 fusion.52
  86.3 0.6 compare_convert_fusion
  87.1 24.5 %all-to-all-done = f32[2,8,64,256]{3,2,0,1:T(8,128)S(1)} async-done(((f32[2,8,64,256]{3,2,0,1:T(8,128)}), f32[2,8,64,256]{3,2,0,1:T(8,128)S(1)}, u32[]{:S(2)}, u32[]{:S(2)}) %all-to-all-start) | async-done | bytes 1048608 | tf_op jit(solution)/shard_map/all_to_all | solution.py:50
  111.6 0.8 copy.17
  112.4 2.6 %gather_fusion.1 = f32[512,2,256]{2,1,0:T(2,128)S(1)} fusion(f32[2,512,256]{2,0,1:T(2,128)S(1)} %bitcast.83, s32[1024]{0:T(1024)S(1)} %pad_clamp_fusion), kind=kCustom, calls=%fused_computation.1 | custom fusion | bytes 2099200 | tf_op jit(solution)/shard_map/jit(_take)/gather | solution.py:57
  115.3 1.0 pad_maximum_fusion.2
  116.3 18.6 %all-reduce.2.cloned.1.call-done = f32[2,512,256]{2,1,0:T(8,128)} async-done(((f32[2,512,256]{2,1,0:T(8,128)}), f32[2,512,256]{2,1,0:T(8,128)}) %all-reduce.2.cloned.1.call-update) | async-done | bytes 1048592 | tf_op jit(solution)/shard_map/psum | solution.py:64
  135.0 2.3 %copy.23 = f32[2,512,256]{2,1,0:T(8,128)} copy(f32[2,512,256]{2,1,0:T(8,128)} %all-reduce.2.cloned.1.call-done) | data formatting | bytes 2097152
  (36 shorter events, 3.3 us)
Async XLA Ops:
  6.5 4.6 %copy-start.4 = (bf16[2,1024,1024]{2,1,0:T(8,128)(2,1)S(1)}, bf16[2,1024,1024]{2,1,0:T(8,128)(2,1)}, u32[]{:S(2)}) copy-start(bf16[2,1024,1024]{2,1,0:T(8,128)(2,1)} %param.11) | copy-start | bytes 12582916
  6.5 4.6 %copy-start.6 = (bf16[1,2,512,1024]{3,2,1,0:T(8,128)(2,1)S(1)}, bf16[1,2,512,1024]{3,2,1,0:T(8,128)(2,1)}, u32[]{:S(2)}) copy-start(bf16[1,2,512,1024]{3,2,1,0:T(8,128)(2,1)} %param.8) | copy-start | bytes 6291460
  13.8 3.6 %copy-start.5 = (bf16[2,1024,1024]{2,1,0:T(8,128)(2,1)S(1)}, bf16[2,1024,1024]{2,1,0:T(8,128)(2,1)}, u32[]{:S(2)}) copy-start(bf16[2,1024,1024]{2,1,0:T(8,128)(2,1)} %param.11) | copy-start | bytes 12582916
  13.8 4.1 %copy-start.8 = (f32[512,1024]{1,0:T(8,128)S(1)}, f32[512,1024]{1,0:T(8,128)}, u32[]{:S(2)}) copy-start(f32[512,1024]{1,0:T(8,128)} %fusion) | copy-start | bytes 6291460
  19.2 4.6 %copy-start.3 = (s32[1024]{0:T(1024)S(1)}, s32[1024]{0:T(1024)}, u32[]{:S(2)}) copy-start(s32[1024]{0:T(1024)} %param.10) | copy-start | bytes 12292
  19.7 49.9 %collective-permute-start = (bf16[2,512,512]{2,1,0:T(8,128)(2,1)S(1)}, bf16[2,512,512]{2,1,0:T(8,128)(2,1)}, u32[]{:S(2)}, u32[]{:S(2)}) collective-permute-start(bf16[2,512,512]{2,1,0:T(8,128)(2,1)S(1)} %get-tuple-element.5), channel_id=1, source_target_pairs={{0,8},{2,10},{4,12},{6,14},{8,0},{10,2},{12,4},{14,6},{1,9},{3,11}... | collective-permute-start | bytes 3145736 | tf_op jit(solution)/shard_map/ppermute | solution.py:10
  74.3 1.3 copy-start
  78.8 6.9 %copy-start.7 = (s32[1,4]{1,0:T(1,128)S(1)}, s32[1,4]{1,0:T(1,128)}, u32[]{:S(2)}) copy-start(s32[1,4]{1,0:T(1,128)} %param.9) | copy-start | bytes 52
  78.8 8.1 %copy-start.2 = (s32[512]{0:T(512)S(1)}, s32[512]{0:T(512)}, u32[]{:S(2)}) copy-start(s32[512]{0:T(512)} %param.15) | copy-start | bytes 6148
  78.8 8.1 %copy-start.1 = (f32[16,2,256]{2,1,0:T(2,128)S(1)}, f32[16,2,256]{2,1,0:T(2,128)}, u32[]{:S(2)}) copy-start(f32[16,2,256]{2,1,0:T(2,128)} %param.14) | copy-start | bytes 98308
  79.9 31.7 %all-to-all-start = ((f32[2,8,64,256]{3,2,0,1:T(8,128)}), f32[2,8,64,256]{3,2,0,1:T(8,128)S(1)}, u32[]{:S(2)}, u32[]{:S(2)}) async-start(f32[2,8,64,256]{3,2,0,1:T(8,128)} %pad_maximum_fusion.1), calls=%async_computation | async-start | bytes 2097152 | tf_op jit(solution)/shard_map/all_to_all | solution.py:50
  85.7 49.3 %all-reduce.2.cloned.1.call-start = ((), (), s32[]{:S(2)}) async-start(), calls=%async_computation.1 | async-start | bytes 2097152 | tf_op jit(solution)/shard_map/psum | solution.py:64
Sparse Core Ops, SparseCore 0:
  116.5 18.4 all-reduce.1
where the time goes:
time: 145 us; the launch traced here: 144 us
  waiting for transfers between devices  54.1 us (37%)
  local copies, waits for them, and re-layouts  38.3 us (26%)
  matrix products  19.1 us (13%)
  between operations  13.7 us (9%)
  starting transfers between devices  9.93 us (7%)
  other arithmetic  9.01 us (6%)
    gather x1, local copies, waits for them, and re-layouts, on_device(): reordered = jnp.take(branch_second, inverse, axis=1)  27.6 us
    all_to_all x1, waiting for transfers between devices, on_device(): lax.all_to_all(contracted.reshape(2, stem_size, block_rows, contracted.sh...  24.5 us
    psum x1, waiting for transfers between devices, on_device(): return lax.psum(total, 'cuts')  18.6 us
    ppermute x1, waiting for transfers between devices, swapped(): return lax.ppermute(value, axis, pairs)  10.9 us
    dot_general x3, matrix products, complex_dot(): jnp.dot(operand[1], matrix[1], preferred_element_type=jnp.float32)  6.33 us
    all_to_all x1, starting transfers between devices, on_device(): lax.all_to_all(contracted.reshape(2, stem_size, block_rows, contracted.sh...  5.77 us
    dot_general x3, matrix products, complex_dot(): jnp.dot(operand[0], matrix[0], preferred_element_type=jnp.float32)  5.36 us
    scatter x1, local copies, waits for them, and re-layouts, on_device(): jnp.zeros_like(index_order).at[index_order]  4.49 us
  transfers between devices with their start and end apart: 3, of which 3 were waited for; matrix products, arithmetic and copies ran while one was open for 25% of the time, Pallas kernels for 0%

commit v1 on v0

v1 whole, which is shorter than its diff:
```python
import jax
import jax.numpy as jnp
from jax import lax
from jax.sharding import PartitionSpec as P


def dot32(left, right):
    return jnp.dot(left, right, preferred_element_type=jnp.float32)


def turned(matrix):
    half = matrix.shape[1] // 2
    return jnp.concatenate([-matrix[:, half:], matrix[:, :half]], axis=1)


def on_device(
    stem, edge_values, index_order, branch_first, branch_second, branch_third, edge_table, picks
):
    stem_size = lax.axis_size("stem")
    cut_size = lax.axis_size("cuts")
    half_size = stem_size // 2
    top_bit = lax.axis_index("stem") // half_size
    core = lax.axis_index("cuts")
    width = branch_first.shape[1]
    half_width = width // 2
    rows_dev = stem.shape[2]
    half_rows = rows_dev // 2
    block_rows = rows_dev // stem_size
    cols = branch_third.shape[2]
    swap = [(source, source ^ 1) for source in range(cut_size)]

    other_stem = lax.ppermute(stem, "cuts", swap)
    other_edges = lax.ppermute(edge_values, "cuts", swap)

    third_cat = jnp.concatenate([branch_third[0], branch_third[1]], axis=1)
    weight = dot32(branch_second[0], third_cat) + dot32(branch_second[1], turned(third_cat))
    powers = 2 ** jnp.arange(edge_values.shape[1], dtype=jnp.int32)

    def scaled(edges):
        code = jnp.sum(edges[0] * powers)
        factor = lax.dynamic_index_in_dim(edge_table, code, 0, keepdims=False)
        real, imag = weight[:, :cols], weight[:, cols:]
        return jnp.concatenate(
            [real * factor[0] - imag * factor[1], real * factor[1] + imag * factor[0]], axis=1
        ).astype(jnp.bfloat16)

    rows_of = lax.broadcasted_iota(jnp.int32, (half_width, width), 0) + top_bit * half_width
    chosen = (rows_of == index_order[None, :]).astype(jnp.bfloat16)
    first_half = lax.dynamic_slice_in_dim(branch_first, core * half_width, half_width, axis=2)

    total = None
    for one_stem, edges in ((stem, edge_values), (other_stem, other_edges)):
        ordered = dot32(chosen, scaled(edges)).astype(jnp.bfloat16)
        merged = (dot32(first_half[0], ordered) + dot32(first_half[1], turned(ordered))).astype(
            jnp.bfloat16
        )
        part = dot32(one_stem[0, 0], merged) + dot32(one_stem[0, 1], turned(merged))
        total = part if total is None else total + part
    sent = total.astype(jnp.bfloat16).reshape(stem_size, block_rows, 2 * cols)
    own = lax.all_to_all(sent, "stem", split_axis=0, concat_axis=0, tiled=True)
    own = own.reshape(rows_dev, 2 * cols)
    other = lax.ppermute(own, "cuts", swap)
    place = lax.broadcasted_iota(jnp.int32, (rows_dev, rows_dev), 1) % half_rows
    pick_own = (place + core * half_rows == picks[:, None]).astype(jnp.bfloat16)
    pick_other = (place + (1 - core) * half_rows == picks[:, None]).astype(jnp.bfloat16)
    rows = dot32(pick_own, own) + dot32(pick_other, other)
    return jnp.stack([rows[:, :cols], rows[:, cols:]])


def solution(mesh):
    return jax.shard_map(
        on_device,
        mesh=mesh,
        in_specs=(
            P(("groups", "cuts"), None, "stem", None),
            P(("groups", "cuts"), None),
            P(),
            P(),
            P(),
            P(),
            P(),
            P("stem"),
        ),
        out_specs=P(None, ("groups", "stem"), None),
        check_vma=False,
    )
```

time: 145 us -> 53.7 us (0.37)
  waiting for transfers between devices: 54.1 us -> 1.41 us
  local copies, waits for them, and re-layouts: 38.3 us -> 5.04 us
  blocking collectives: 0 us -> 21.8 us
  between operations: 13.7 us -> 4.13 us
  starting transfers between devices: 9.93 us -> 0.51 us
  other arithmetic: 9.01 us -> 4.85 us
  matrix products: 19.1 us -> 15.5 us
    gather x2 -> x0, local copies, waits for them, and re-layouts: 30.2 us -> none  [the longest x1 27.6 us: on_device(): reordered = jnp.take(branch_second, inverse, axis=1)]
    all_to_all x1 -> x0, waiting for transfers between devices: 24.5 us -> none  [on_device(): lax.all_to_all(contracted.reshape(2, stem_size, block_rows, contracted.sh...]
    all_to_all x0 -> x1, blocking collectives: none -> 21.8 us  [on_device(): own = lax.all_to_all(sent, 'stem', split_axis=0, concat_axis=0, tiled=True)]
    psum x1 -> x0, waiting for transfers between devices: 18.6 us -> none  [on_device(): return lax.psum(total, 'cuts')]
    ppermute x1 -> x3, waiting for transfers between devices: 10.9 us -> 1.41 us  [the longest x1 1.41 us: on_device(): other = lax.ppermute(own, 'cuts', swap)]
    all_to_all x1 -> x0, starting transfers between devices: 5.77 us -> none  [on_device(): lax.all_to_all(contracted.reshape(2, stem_size, block_rows, contracted.sh...]
    select_n x6 -> x0, other arithmetic: 5.48 us -> none  [the longest x1 2.63 us: on_device(): reordered = jnp.take(branch_second, inverse, axis=1)]
    scatter x1 -> x0, local copies, waits for them, and re-layouts: 4.49 us -> none  [on_device(): jnp.zeros_like(index_order).at[index_order]]
  transfers between devices with their start and end apart: 3 -> 3, of which waited for: 3 -> 1; matrix products, arithmetic and copies ran while one was open for 25% -> 32% of each run, Pallas kernels for 0% -> 0%
where the time goes in v1:
time: 53.7 us; the launch traced here: 53.2 us
  blocking collectives  21.8 us (41%)
  matrix products  15.5 us (29%)
  local copies, waits for them, and re-layouts  5.04 us (9%)
  other arithmetic  4.85 us (9%)
  between operations  4.13 us (8%)
  waiting for transfers between devices  1.41 us (3%)
    all_to_all x1, blocking collectives, on_device(): own = lax.all_to_all(sent, 'stem', split_axis=0, concat_axis=0, tiled=True)  21.8 us
    dot_general x14, matrix products, dot32(): return jnp.dot(left, right, preferred_element_type=jnp.float32)  15.5 us
    unnamed x10, local copies, waits for them, and re-layouts  2.92 us
    reduce_sum x2, other arithmetic, scaled(): code = jnp.sum(edges[0] * powers)  1.94 us
    ppermute x1, waiting for transfers between devices, on_device(): other = lax.ppermute(own, 'cuts', swap)  1.41 us
    neg x5, other arithmetic, turned(): return jnp.concatenate([-matrix[:, half:], matrix[:, :half]], axis=1)  1.29 us
    squeeze x1, local copies, waits for them, and re-layouts, on_device(): third_cat = jnp.concatenate([branch_third[0], branch_third[1]], axis=1)  1.27 us
  transfers between devices with their start and end apart: 3, of which 1 were waited for; matrix products, arithmetic and copies ran while one was open for 32% of the time, Pallas kernels for 0%

profile of v1, /device:TPU:0, one launch (start us, length us, event | category | flops | bytes accessed | tf_op | source)
XLA Modules:
  0.0 53.2 jit_solution(9173139618803918810)
XLA Ops:
  0.0 0.5 collective-permute-start
  0.5 1.3 %fusion.82 = s32[]{:T(128)} fusion(s32[1,4]{1,0:T(1,128)} %param.9), kind=kLoop, calls=%fused_computation.115 | loop fusion | flops 115 | bytes 20 | tf_op jit(solution)/shard_map/reduce_sum | solution.py:40
  1.8 1.1 %fusion.91 = bf16[1024,256]{1,0:T(8,128)(2,1)S(1)} fusion(bf16[2,1024,256]{2,1,0:T(8,128)(2,1)} %param.13), kind=kLoop, calls=%fused_computation.124 | loop fusion | flops 262144 | bytes 1048576 | tf_op jit(solution)/shard_map/neg | solution.py:13
  2.9 1.3 %slice_bitcast_fusion.6 = (bf16[1024,256]{1,0:T(8,128)(2,1)S(1)}, bf16[1024,256]{1,0:T(8,128)(2,1)S(1)}) fusion(bf16[2,1024,256]{2,1,0:T(8,128)(2,1)} %param.13), kind=kLoop, calls=%fused_computation.75 | loop fusion | bytes 2097152 | tf_op jit(solution)/shard_map/squeeze | solution.py:35
  6.2 3.0 %fusion.4 = f32[512,1024]{1,0:T(8,128)S(1)} fusion(bf16[2,1024,1024]{2,1,0:T(8,128)(2,1)} %param.12, bf16[1024,256]{1,0:T(8,128)(2,1)S(1)} %get-tuple-element.18, bf16[1024,256]{1,0:T(8,128)(2,1)S(1)} %fusion.91), kind=kOutput, calls=%fused_computation.4 | convolution fusion | flops 1075838976 | bytes 5242880 | tf_op jit(solution)/shard_map/dot_general | solution.py:8
  9.2 1.3 %add_bitcast_fusion = f32[1024,512]{0,1:T(8,128)S(1)} fusion(f32[512,1024]{1,0:T(8,128)S(1)} %fusion.4, bf16[2,1024,1024]{2,1,0:T(8,128)(2,1)S(1)} %copy-done.2, bf16[1024,256]{1,0:T(8,128)(2,1)S(1)} %get-tuple-element.17, bf16[1024,256]{1,0:T(8,128)(2,1)S(1)} %get-tuple-element.18), kind=kOutput, calls=%fused_computation.10 | convolution fusion | flops 1076363264 | bytes 7340032 | tf_op jit(solution)/shard_map/dot_general | solution.py:8
  10.5 0.6 %fusion.81 = s32[]{:T(128)} fusion(s32[1,4]{1,0:T(1,128)S(1)} %collective-permute-done), kind=kLoop, calls=%fused_computation.113 | loop fusion | flops 115 | bytes 20 | tf_op jit(solution)/shard_map/reduce_sum | solution.py:40
  13.1 0.8 %constant_dynamic-slice_fusion = (f32[1,1,256]{2,1,0:T(1,128)S(1)}, f32[1,1,256]{2,1,0:T(1,128)S(1)}, f32[1,1,256]{2,1,0:T(1,128)S(1)}, f32[1,1,256]{2,1,0:T(1,128)S(1)}) fusion(f32[16,2,256]{2,1,0:T(2,128)} %param.14, s32[]{:T(128)S(6)} %select_n.67, s32[]{:T(128)S(6)} %select_n.66, s32[]{:T(128)S(6)} %add.92), kind=kLoop, calls=%fused_computation.102 | loop fusion | bytes 8204 | tf_op jit(solution)/shard_map/slice | solution.py:44
  13.9 0.6 %subtract_convert_fusion = (bf16[1024,256]{0,1:T(8,128)(2,1)S(1)}, bf16[1024,256]{0,1:T(8,128)(2,1)S(1)}, bf16[1024,256]{0,1:T(8,128)(2,1)S(1)}, bf16[1024,256]{0,1:T(8,128)(2,1)S(1)}) fusion(f32[1024,512]{0,1:T(8,128)S(1)} %add_bitcast_fusion, f32[256]{0:T(256)S(1)} %bitcast.67, f32[256]{0:T(256)S(1)} %bitcast.65, f32[256]{0:T(256)S(1)} %bitcast.66, ...), kind=kLoop, calls=%fused_computation.52 | loop fusion | flops 4194304 | bytes 4198400 | tf_op jit(solution)/shard_map/convert
  14.6 0.8 %fusion.16 = bf16[512,512]{0,1:T(8,128)(2,1)S(1)} fusion(bf16[1024,256]{0,1:T(8,128)(2,1)S(1)} %get-tuple-element.6, bf16[1024,256]{0,1:T(8,128)(2,1)S(1)} %get-tuple-element.5, s32[1024]{0:T(1024)S(1)} %copy-done.4, s32[512]{0:T(512)S(1)} %iota_add_fusion), kind=kOutput, calls=%fused_computation.20 | convolution fusion | flops 539754496 | bytes 1579008 | tf_op jit(solution)/shard_map/dot_general | solution.py:8
  15.5 0.8 %fusion.13 = bf16[512,512]{0,1:T(8,128)(2,1)S(1)} fusion(bf16[1024,256]{0,1:T(8,128)(2,1)S(1)} %get-tuple-element.9, bf16[1024,256]{0,1:T(8,128)(2,1)S(1)} %get-tuple-element.10, s32[1024]{0:T(1024)S(1)} %copy-done.4, s32[512]{0:T(512)S(1)} %iota_add_fusion), kind=kOutput, calls=%fused_computation.19 | convolution fusion | flops 539754496 | bytes 1579008 | tf_op jit(solution)/shard_map/dot_general | solution.py:8
  16.3 1.3 %copy-done = bf16[2,1024,1024]{2,1,0:T(8,128)(2,1)S(1)} copy-done((bf16[2,1024,1024]{2,1,0:T(8,128)(2,1)S(1)}, bf16[2,1024,1024]{2,1,0:T(8,128)(2,1)}, u32[]{:S(2)}) %copy-start) | copy-done | bytes 4194328
  17.6 0.7 %fusion.53 = f32[1024,512]{0,1:T(8,128)S(1)} fusion(bf16[512,512]{0,1:T(8,128)(2,1)S(1)} %fusion.16, bf16[2,1024,1024]{2,1,0:T(8,128)(2,1)S(1)} %copy-done, s32[]{:T(128)S(6)} %select_n.58), kind=kOutput, calls=%fused_computation.62 | convolution fusion | flops 536870912 | bytes 3670020 | tf_op jit(solution)/shard_map/dot_general | solution.py:8
  18.4 0.8 %add_convert_fusion = bf16[1024,512]{0,1:T(8,128)(2,1)S(1)} fusion(f32[1024,512]{0,1:T(8,128)S(1)} %fusion.53, bf16[2,1024,1024]{2,1,0:T(8,128)(2,1)S(1)} %copy-done, s32[]{:T(128)S(6)} %add.92, s32[]{:T(128)S(6)} %select_n.58, bf16[512,256]{0,1:T(8,128)(2,1)S(1)} %get-tuple-element.20, bf16[512,256]{0,1:T(8,128)(2,1)S(1)} %get-tuple-element.19), kind=kOutput, calls=%fused_computation.8 | convolution fusion | flops 538968064 | bytes 4718600 | tf_op jit(solution)/shard_map/dot_general | solution.py:8
  19.3 0.7 %fusion.54 = f32[1024,512]{0,1:T(8,128)S(1)} fusion(bf16[512,512]{0,1:T(8,128)(2,1)S(1)} %fusion.13, bf16[2,1024,1024]{2,1,0:T(8,128)(2,1)S(1)} %copy-done, s32[]{:T(128)S(6)} %select_n.58), kind=kOutput, calls=%fused_computation.63 | convolution fusion | flops 536870912 | bytes 3670020 | tf_op jit(solution)/shard_map/dot_general | solution.py:8
  20.0 0.8 %add_convert_fusion.1 = bf16[1024,512]{0,1:T(8,128)(2,1)S(1)} fusion(f32[1024,512]{0,1:T(8,128)S(1)} %fusion.54, bf16[2,1024,1024]{2,1,0:T(8,128)(2,1)S(1)} %copy-done, s32[]{:T(128)S(6)} %add.92, s32[]{:T(128)S(6)} %select_n.58, bf16[512,256]{0,1:T(8,128)(2,1)S(1)} %get-tuple-element.22, bf16[512,256]{0,1:T(8,128)(2,1)S(1)} %get-tuple-element.21), kind=kOutput, calls=%fused_computation.9 | convolution fusion | flops 538968064 | bytes 4718600 | tf_op jit(solution)/shard_map/dot_general | solution.py:8
  20.9 1.5 %copy-done.3 = bf16[1,2,512,1024]{3,2,1,0:T(8,128)(2,1)S(1)} copy-done((bf16[1,2,512,1024]{3,2,1,0:T(8,128)(2,1)S(1)}, bf16[1,2,512,1024]{3,2,1,0:T(8,128)(2,1)}, u32[]{:S(2)}) %copy-start.3) | copy-done | bytes 2097176
  22.4 0.7 %fusion.42 = f32[512,512]{0,1:T(8,128)S(1)} fusion(bf16[1024,512]{0,1:T(8,128)(2,1)S(1)} %add_convert_fusion.1, bf16[1,2,512,1024]{3,2,1,0:T(8,128)(2,1)S(1)} %copy-done.3), kind=kOutput, calls=%fused_computation.49 | convolution fusion | flops 536870912 | bytes 3145728 | tf_op jit(solution)/shard_map/dot_general | solution.py:8
  23.1 0.7 %convolution_add_fusion.2 = f32[512,512]{0,1:T(8,128)S(1)} fusion(f32[512,512]{0,1:T(8,128)S(1)} %fusion.42, bf16[1024,256]{0,1:T(8,128)(2,1)S(1)} %get-tuple-element.16, bf16[1024,256]{0,1:T(8,128)(2,1)S(1)} %get-tuple-element.15, bf16[1,2,512,1024]{3,2,1,0:T(8,128)(2,1)S(1)} %copy-done.3), kind=kOutput, calls=%fused_computation.18 | convolution fusion | flops 539230208 | bytes 4194304 | tf_op jit(solution)/shard_map/dot_general | solution.py:8
  23.9 2.0 %fusion.22 = f32[512,512]{0,1:T(8,128)S(1)} fusion(bf16[1,2,512,1024]{3,2,1,0:T(8,128)(2,1)} %collective-permute-done.1, bf16[1024,256]{0,1:T(8,128)(2,1)S(1)} %get-tuple-element.14, bf16[1024,256]{0,1:T(8,128)(2,1)S(1)} %get-tuple-element.13), kind=kOutput, calls=%fused_computation.25 | convolution fusion | flops 538968064 | bytes 3145728 | tf_op jit(solution)/shard_map/dot_general | solution.py:8
  25.9 2.0 %fusion.19 = bf16[512,512]{0,1:T(8,128)(2,1)S(1)} fusion(f32[512,512]{0,1:T(8,128)S(1)} %convolution_add_fusion.2, f32[512,512]{0,1:T(8,128)S(1)} %fusion.22, bf16[1024,512]{0,1:T(8,128)(2,1)S(1)} %add_convert_fusion, bf16[1,2,512,1024]{3,2,1,0:T(8,128)(2,1)} %collective-permute-done.1), kind=kOutput, calls=%fused_computation.21 | convolution fusion | flops 537657344 | bytes 4718592 | tf_op jit(solution)/shard_map/dot_general | solution.py:8
  27.9 21.8 %all_to_all.5 = bf16[8,64,512]{2,1,0:T(8,128)(2,1)S(1)} all-to-all(bf16[8,64,512]{2,1,0:T(8,128)(2,1)S(1)} %bitcast.62), channel_id=1, replica_groups=mesh['groups'=2,'stem'=8,'cuts'=2] {'stem'}, dimensions={0} | all-to-all | bytes 1048576 | tf_op jit(solution)/shard_map/all_to_all | solution.py:60
  50.2 1.4 %collective-permute-done.2 = bf16[512,512]{1,0:T(8,128)(2,1)S(1)} collective-permute-done((bf16[512,512]{1,0:T(8,128)(2,1)S(1)}, bf16[512,512]{1,0:T(8,128)(2,1)S(1)}, u32[]{:S(2)}, u32[]{:S(2)}) %collective-permute-start.2) | collective-permute-done | bytes 524320 | tf_op jit(solution)/shard_map/ppermute | solution.py:62
  52.2 1.0 %pad_maximum_fusion = f32[2,512,256]{2,1,0:T(8,128)} fusion(f32[1,512,256]{2,1,0:T(8,128)S(1)} %get-tuple-element.12, f32[1,512,256]{2,1,0:T(8,128)S(1)} %get-tuple-element.11), kind=kLoop, calls=%fused_computation.47 | loop fusion | flops 262144 | bytes 2097152 | tf_op jit(solution)/shard_map/stack | solution.py:67
  (22 shorter events, 1.4 us)
Async XLA Ops:
  0.0 10.5 %collective-permute-start = (s32[1,4]{1,0:T(1,128)}, s32[1,4]{1,0:T(1,128)S(1)}, u32[]{:S(2)}, u32[]{:S(2)}) collective-permute-start(s32[1,4]{1,0:T(1,128)} %param.9), channel_id=1, source_target_pairs={{0,1},{1,0},{2,3},{3,2},{4,5},{5,4},{6,7},{7,6},{8,9},{9,8},{10,11... | collective-permute-start | bytes 56 | tf_op jit(solution)/shard_map/ppermute | solution.py:33
  0.5 23.4 %collective-permute-start.1 = (bf16[1,2,512,1024]{3,2,1,0:T(8,128)(2,1)}, bf16[1,2,512,1024]{3,2,1,0:T(8,128)(2,1)}, u32[]{:S(2)}, u32[]{:S(2)}) collective-permute-start(bf16[1,2,512,1024]{3,2,1,0:T(8,128)(2,1)} %param.8), channel_id=1, source_target_pairs={{0,1},{1,0},{2,3},{3,2},{4,5},{5,4},{6,7},{7,6},{8,9},{9,8},{10,11... | collective-permute-start | bytes 6291464 | tf_op jit(solution)/shard_map/ppermute | solution.py:32
  6.1 3.1 %copy-start.2 = (bf16[2,1024,1024]{2,1,0:T(8,128)(2,1)S(1)}, bf16[2,1024,1024]{2,1,0:T(8,128)(2,1)}, u32[]{:S(2)}) copy-start(bf16[2,1024,1024]{2,1,0:T(8,128)(2,1)} %param.12) | copy-start | bytes 12582916
  13.9 0.7 %copy-start.4 = (s32[1024]{0:T(1024)S(1)}, s32[1024]{0:T(1024)}, u32[]{:S(2)}) copy-start(s32[1024]{0:T(1024)} %param.10) | copy-start | bytes 12292
  15.4 2.2 %copy-start = (bf16[2,1024,1024]{2,1,0:T(8,128)(2,1)S(1)}, bf16[2,1024,1024]{2,1,0:T(8,128)(2,1)}, u32[]{:S(2)}) copy-start(bf16[2,1024,1024]{2,1,0:T(8,128)(2,1)} %param.11) | copy-start | bytes 12582916
  20.8 1.6 %copy-start.3 = (bf16[1,2,512,1024]{3,2,1,0:T(8,128)(2,1)S(1)}, bf16[1,2,512,1024]{3,2,1,0:T(8,128)(2,1)}, u32[]{:S(2)}) copy-start(bf16[1,2,512,1024]{3,2,1,0:T(8,128)(2,1)} %param.8) | copy-start | bytes 6291460
  25.9 23.8 %copy-start.1 = (s32[512]{0:T(512)S(1)}, s32[512]{0:T(512)}, u32[]{:S(2)}) copy-start(s32[512]{0:T(512)} %param.15) | copy-start | bytes 6148
  49.7 1.9 %collective-permute-start.2 = (bf16[512,512]{1,0:T(8,128)(2,1)S(1)}, bf16[512,512]{1,0:T(8,128)(2,1)S(1)}, u32[]{:S(2)}, u32[]{:S(2)}) collective-permute-start(bf16[512,512]{1,0:T(8,128)(2,1)S(1)} %bitcast.63), channel_id=1, source_target_pairs={{0,1},{1,0},{2,3},{3,2},{4,5},{5,4},{6,7},{7,6},{8,9},{9,8},{10,11... | collective-permute-start | bytes 1572872 | tf_op jit(solution)/shard_map/ppermute | solution.py:62
